TPU v7x, 32 devices: a whole 2x2x4 slice. The times are simulated.
32 devices in a mesh: loss: 4 (over x, core), tower: 4 (over z), pipe: 2 (over y).
Axes of the slice: x: 2, y: 2, z: 4, core: 2. Of those that a mesh axis runs over, the one named last changes fastest.
Arguments:
- image_feats: bfloat16 [4, 2, 24, 1536], P('loss', 'pipe', None, 'tower'), may hold values from -6 to 6
- text_tokens: bfloat16 [4, 2, 24, 64, 1152], P('loss', 'pipe', None, None, 'tower'), may hold values from -6 to 6
- lengths: int32 [4, 2, 24], P('loss', 'pipe'), may hold values from 1 to 64, as said below
- w_image: bfloat16 [1536, 1536], P('tower'), may hold values from -0.15625 to 0.15625
- w_text: bfloat16 [1152, 1536], P('tower'), may hold values from -0.1875 to 0.1875
- logit_scale: float32 [1], replicated, may hold values from 24 to 48
- logit_bias: float32 [1], replicated, may hold values from -4 to -2
Outputs:
- image_grad: float32 [4, 2, 24, 1536], P('loss', 'pipe', 'tower')
- text_grad: float32 [4, 2, 24, 1536], P('loss', 'pipe', 'tower')
Inputs may be any that keep to these rules, and one draw needn't show every extreme that they name: `lengths`: in every group of 24 captions one caption has 64 tokens and one has a single token.
All inputs are finite; a program needn't handle non-finite values.
Results may differ from a plain program's by a relative error of at most 0.0036.
The roundings to bfloat16 on the way count: a program that leaves them out, or rounds other values in their place, can miss the bound.
Values may be sent and summed in bfloat16 or wider, within the bound.
A program may use at most 64 MiB of HBM per device.

v0:
```python
import jax
import jax.numpy as jnp
from jax import lax
from jax.sharding import PartitionSpec as P


def normalize(raw):
    return raw * lax.rsqrt(jnp.sum(raw * raw, axis=-1, keepdims=True) + 1e-06)


def pair_terms(image_unit, texts, image_ids, text_ids, scale, shift):
    scores = jnp.dot(image_unit, texts.T, preferred_element_type=jnp.float32)
    match = (image_ids[:, None] == text_ids[None, :]).astype(jnp.float32)
    return (jax.nn.sigmoid(scale * scores + shift) - match).astype(jnp.bfloat16)


def per_device(image_feats, text_tokens, lengths, w_image, w_text, logit_scale, logit_bias):
    group = image_feats.shape[2]
    emb = w_image.shape[1]
    images = image_feats.reshape(group, image_feats.shape[3])
    words = text_tokens.reshape(group, text_tokens.shape[3], text_tokens.shape[4])
    counts = lengths.reshape(group)
    places = lax.broadcasted_iota(jnp.int32, (group, words.shape[1]), 1)
    keep = (places < counts[:, None]).astype(jnp.bfloat16)
    summed = jnp.einsum("bl,bld->bd", keep, words, preferred_element_type=jnp.float32)
    pooled = (summed / counts.astype(jnp.float32)[:, None]).astype(jnp.bfloat16)
    image_raw = lax.psum(jnp.dot(images, w_image, preferred_element_type=jnp.float32), "tower")
    towers = lax.axis_size("tower")
    sub = group // towers
    text_raw = lax.psum_scatter(
        jnp.dot(pooled, w_text, preferred_element_type=jnp.float32),
        "tower",
        scatter_dimension=0,
        tiled=True,
    )
    image_unit = normalize(image_raw).astype(jnp.bfloat16)
    text_unit = normalize(text_raw).astype(jnp.bfloat16)
    scale = logit_scale[0]
    shift = logit_bias[0]
    loss_at = lax.axis_index("loss")
    pipe_at = lax.axis_index("pipe")
    tower_at = lax.axis_index("tower")
    pipes = lax.axis_size("pipe")
    image_ids = (loss_at * pipes + pipe_at) * group + lax.iota(jnp.int32, group)
    texts = lax.all_gather(text_unit, ("loss", "pipe"), axis=0, tiled=True)
    spots = lax.iota(jnp.int32, texts.shape[0])
    text_ids = spots // sub * group + tower_at * sub + spots % sub
    grads = pair_terms(image_unit, texts, image_ids, text_ids, scale, shift)
    image_term = scale * jnp.dot(grads, texts, preferred_element_type=jnp.float32)
    text_grad = lax.psum_scatter(
        scale
        * lax.dot_general(
            grads, image_unit, (((0,), (0,)), ((), ())), preferred_element_type=jnp.float32
        ),
        ("loss", "pipe"),
        scatter_dimension=0,
        tiled=True,
    )
    image_grad = lax.psum_scatter(image_term, "tower", scatter_dimension=0, tiled=True)
    return (image_grad.reshape(1, 1, sub, emb), text_grad.reshape(1, 1, sub, emb))


def solution(mesh):
    return jax.shard_map(
        per_device,
        mesh=mesh,
        in_specs=(
            P("loss", "pipe", None, "tower"),
            P("loss", "pipe", None, None, "tower"),
            P("loss", "pipe", None),
            P("tower", None),
            P("tower", None),
            P(),
            P(),
        ),
        out_specs=(P("loss", "pipe", "tower", None), P("loss", "pipe", "tower", None)),
        check_vma=False,
    )
```

profile of v0, /device:TPU:1, one launch (start us, length us, event | category | flops | bytes accessed | tf_op | source)
XLA Modules:
  0.0 116.7 jit_solution(13100694398209393492)
XLA Ops:
  7.2 0.8 bitcast_convert_fusion
  8.0 0.7 fusion.20
  8.8 1.6 %fusion.3 = f32[24,1,288]{2,1,0:T(1,128)S(1)} fusion(bf16[1,1,24,64,288]{4,3,2,1,0:T(8,128)(2,1)} %param.8, pred[24,64,1]{1,0,2:T(8,128)(4,1)S(1)} %fusion.20), kind=kOutput, calls=%fused_computation.2 | convolution fusion | flops 884736 | bytes 913920 | tf_op jit(solution)/shard_map/bl,bld->bd/dot_general | solution.py:25
  10.3 0.3 fusion.15
  10.7 12.8 %fusion = f32[8,1536]{1,0:T(8,128)S(1)} fusion(f32[24,1536]{1,0:T(8,128)S(1)} %fusion.15), kind=kCustom, calls=%all-reduce-scatter | all-reduce-scatter fusion | flops 49153 | bytes 197120
  23.5 2.0 %collective-permute-start = (f32[6,1536]{1,0:T(8,128)S(1)}, f32[6,1536]{1,0:T(8,128)S(1)}, u32[]{:S(2)}, u32[]{:S(2)}) collective-permute-start(f32[6,1536]{1,0:T(8,128)S(1)} %slice), channel_id=1, source_target_pairs={{0,2},{2,4},{4,6},{1,3},{3,5},{5,7},{8,10},{10,12},{12,14},{9,11},... | collective-permute-start | bytes 110600
  25.5 0.9 fusion.17
  27.8 0.6 dynamic-slice.8
  28.4 0.7 dynamic-slice.16
  30.8 19.7 %all-gather = bf16[8,6,1536]{2,1,0:T(8,128)(2,1)S(1)} all-gather(bf16[1,6,1536]{2,1,0:T(8,128)(2,1)S(1)} %fusion.14), channel_id=1, replica_groups=mesh['loss'=4,'tower'=4,'pipe'=2] {'loss','pipe'}, dimensions={0}, use_global_device_ids=true | all-gather | bytes 165888 | tf_op jit(solution)/shard_map/all_gather | solution.py:45
  50.5 10.2 %all-reduce.8.cloned.1.call-done = f32[24,1536]{1,0:T(8,128)} async-done(((f32[24,1536]{1,0:T(8,128)}), f32[24,1536]{1,0:T(8,128)}) %all-reduce.8.cloned.1.call-update) | async-done | bytes 147472 | tf_op jit(solution)/shard_map/psum | solution.py:27
  60.7 1.0 multiply_reduce_fusion
  61.7 1.2 fusion.11
  62.9 0.1 convolution_multiply_fusion.1
  63.0 12.3 %fusion.1 = f32[8,1536]{1,0:T(8,128)S(1)} fusion(f32[24,1536]{1,0:T(8,128)S(1)} %convolution_multiply_fusion.1), kind=kCustom, calls=%all-reduce-scatter.1 | all-reduce-scatter fusion | flops 49153 | bytes 197120
  75.3 1.6 %collective-permute-start.1 = (f32[6,1536]{1,0:T(8,128)S(1)}, f32[6,1536]{1,0:T(8,128)S(1)}, u32[]{:S(2)}, u32[]{:S(2)}) collective-permute-start(f32[6,1536]{1,0:T(8,128)S(1)} %slice.1), channel_id=1, source_target_pairs={{0,2},{2,4},{4,6},{1,3},{3,5},{5,7},{8,10},{10,12},{12,14},{9,11},... | collective-permute-start | bytes 110600
  76.9 1.2 convolution_multiply_fusion
  78.0 23.2 %fusion.2 = f32[8,1536]{1,0:T(8,128)S(1)} fusion(f32[48,1536]{1,0:T(8,128)S(1)} %convolution_multiply_fusion), kind=kCustom, calls=%all-reduce-scatter.2 | all-reduce-scatter fusion | flops 98305 | bytes 344576
  101.2 1.9 %collective-permute-start.2 = (f32[8,1536]{1,0:T(8,128)S(1)}, f32[8,1536]{1,0:T(8,128)S(1)}, u32[]{:S(2)}, u32[]{:S(2)}) collective-permute-start(f32[8,1536]{1,0:T(8,128)S(1)} %fusion.2), channel_id=1, source_target_pairs={{0,1},{1,8},{8,9},{9,16},{16,17},{17,24},{24,25},{2,3},{3,10},{10,... | collective-permute-start | bytes 147464
  103.2 4.6 %collective-permute-start.3 = (f32[6,1536]{1,0:T(8,128)S(1)}, f32[6,1536]{1,0:T(8,128)S(1)}, u32[]{:S(2)}, u32[]{:S(2)}) collective-permute-start(f32[6,1536]{1,0:T(8,128)S(1)} %slice.2), channel_id=1, source_target_pairs={{0,8},{1,9},{8,16},{9,17},{16,24},{17,25},{2,10},{3,11},{10,18},{1... | collective-permute-start | bytes 110600
  107.9 0.7 copy.13
  108.6 0.3 collective-permute-done.3
  108.9 0.2 concatenate.2
  109.2 0.7 copy.14
  (29 shorter events, 0.7 us)
Async XLA Ops:
  7.2 18.3 %copy-start = (bf16[384,1536]{1,0:T(8,128)(2,1)S(1)}, bf16[384,1536]{1,0:T(8,128)(2,1)}, u32[]{:S(2)}) copy-start(bf16[384,1536]{1,0:T(8,128)(2,1)} %param.10) | copy-start | bytes 3538948
  7.2 3.2 %copy-start.1 = (bf16[288,1536]{1,0:T(8,128)(2,1)S(1)}, bf16[288,1536]{1,0:T(8,128)(2,1)}, u32[]{:S(2)}) copy-start(bf16[288,1536]{1,0:T(8,128)(2,1)} %param.11) | copy-start | bytes 2654212
  7.2 53.5 %all-reduce.8.cloned.1.call-start = ((), (), s32[]{:S(2)}) async-start(), calls=%async_computation | async-start | bytes 294912 | tf_op jit(solution)/shard_map/psum | solution.py:27
  8.8 16.8 %copy-start.2 = (bf16[1,1,24,384]{3,2,1,0:T(8,128)(2,1)S(1)}, bf16[1,1,24,384]{3,2,1,0:T(8,128)(2,1)}, u32[]{:S(2)}) copy-start(bf16[1,1,24,384]{3,2,1,0:T(8,128)(2,1)} %param.7) | copy-start | bytes 55300
  10.6 17.2 %copy-start.4 = (u32[32]{0:T(128)S(1)}, u32[32]{0:T(128)}, u32[]{:S(2)}) copy-start(u32[32]{0:T(128)} %constant.48) | copy-start | bytes 388
  10.6 17.8 %copy-start.3 = (u32[32]{0:T(128)S(1)}, u32[32]{0:T(128)}, u32[]{:S(2)}) copy-start(u32[32]{0:T(128)} %constant.56) | copy-start | bytes 388
  23.5 6.9 %collective-permute-start = (f32[6,1536]{1,0:T(8,128)S(1)}, f32[6,1536]{1,0:T(8,128)S(1)}, u32[]{:S(2)}, u32[]{:S(2)}) collective-permute-start(f32[6,1536]{1,0:T(8,128)S(1)} %slice), channel_id=1, source_target_pairs={{0,2},{2,4},{4,6},{1,3},{3,5},{5,7},{8,10},{10,12},{12,14},{9,11},... | collective-permute-start | bytes 110600
  75.3 32.4 %collective-permute-start.1 = (f32[6,1536]{1,0:T(8,128)S(1)}, f32[6,1536]{1,0:T(8,128)S(1)}, u32[]{:S(2)}, u32[]{:S(2)}) collective-permute-start(f32[6,1536]{1,0:T(8,128)S(1)} %slice.1), channel_id=1, source_target_pairs={{0,2},{2,4},{4,6},{1,3},{3,5},{5,7},{8,10},{10,12},{12,14},{9,11},... | collective-permute-start | bytes 110600
  101.2 7.7 %collective-permute-start.2 = (f32[8,1536]{1,0:T(8,128)S(1)}, f32[8,1536]{1,0:T(8,128)S(1)}, u32[]{:S(2)}, u32[]{:S(2)}) collective-permute-start(f32[8,1536]{1,0:T(8,128)S(1)} %fusion.2), channel_id=1, source_target_pairs={{0,1},{1,8},{8,9},{9,16},{16,17},{17,24},{24,25},{2,3},{3,10},{10,... | collective-permute-start | bytes 147464
  103.2 5.8 %collective-permute-start.3 = (f32[6,1536]{1,0:T(8,128)S(1)}, f32[6,1536]{1,0:T(8,128)S(1)}, u32[]{:S(2)}, u32[]{:S(2)}) collective-permute-start(f32[6,1536]{1,0:T(8,128)S(1)} %slice.2), channel_id=1, source_target_pairs={{0,8},{1,9},{8,16},{9,17},{16,24},{17,25},{2,10},{3,11},{10,18},{1... | collective-permute-start | bytes 110600
Sparse Core Ops, SparseCore 0:
  26.6 34.0 all-reduce.7
where the time goes:
time: 117 us
  blocking collectives  67.9 us (58%)
  between operations  16.9 us (14%)
  waiting for transfers between devices  10.5 us (9%)
  starting transfers between devices  10.1 us (9%)
  matrix products  5.25 us (4%)
  local copies, waits for them, and re-layouts  3.18 us (3%)
  other arithmetic  2.8 us (2%)
    unnamed x3, blocking collectives  48.2 us
    all_gather x1, blocking collectives, per_device(): texts = lax.all_gather(text_unit, ('loss', 'pipe'), axis=0, tiled=True)  19.7 us
    psum x1, waiting for transfers between devices, per_device(): lax.psum(jnp.dot(images, w_image, preferred_element_type=jnp.float32), 't...  10.2 us
    unnamed x4, starting transfers between devices  10.1 us
    unnamed x21, local copies, waits for them, and re-layouts  3.15 us
  transfers between devices with their start and end apart: 5, of which 2 were waited for; matrix products, arithmetic and copies ran while one was open for 24% of the time, Pallas kernels for 0%

commit v1 on v0

--- a/solution.py
+++ b/solution.py
@@ -24,7 +24,10 @@
     keep = (places < counts[:, None]).astype(jnp.bfloat16)
     summed = jnp.einsum("bl,bld->bd", keep, words, preferred_element_type=jnp.float32)
     pooled = (summed / counts.astype(jnp.float32)[:, None]).astype(jnp.bfloat16)
-    image_raw = lax.psum(jnp.dot(images, w_image, preferred_element_type=jnp.float32), "tower")
+    image_raw = jnp.sum(
+        lax.all_gather(jnp.dot(images, w_image, preferred_element_type=jnp.float32), "tower"),
+        axis=0,
+    )
     towers = lax.axis_size("tower")
     sub = group // towers
     text_raw = lax.psum_scatter(

time: 117 us -> 101 us (0.86)
  between operations: 16.9 us -> 3.39 us
  blocking collectives: 67.9 us -> 78.6 us
  waiting for transfers between devices: 10.5 us -> 0.34 us
  matrix products: 5.25 us -> 2.76 us
    all_gather x0 -> x1, blocking collectives: none -> 13.8 us  [per_device(): lax.all_gather(jnp.dot(images, w_image, preferred_element_type=jnp.float3...]
    psum x1 -> x0, waiting for transfers between devices: 10.2 us -> none  [per_device(): lax.psum(jnp.dot(images, w_image, preferred_element_type=jnp.float32), 't...]
    unnamed x3, blocking collectives: 48.2 us -> 43.7 us
    all_gather x1, blocking collectives: 19.7 us -> 21.1 us  [per_device(): texts = lax.all_gather(text_unit, ('loss', 'pipe'), axis=0, tiled=True)]
  transfers between devices with their start and end apart: 5 -> 4, of which waited for: 2 -> 1; matrix products, arithmetic and copies ran while one was open for 24% -> 23% of each run, Pallas kernels for 0% -> 0%
where the time goes in v1:
time: 101 us; the launch traced here: 100 us
  blocking collectives  78.6 us (78%)
  starting transfers between devices  10 us (10%)
  between operations  3.39 us (3%)
  local copies, waits for them, and re-layouts  3.1 us (3%)
  matrix products  2.76 us (3%)
  other arithmetic  1.93 us (2%)
    unnamed x3, blocking collectives  43.7 us
    all_gather x1, blocking collectives, per_device(): texts = lax.all_gather(text_unit, ('loss', 'pipe'), axis=0, tiled=True)  21.1 us
    all_gather x1, blocking collectives, per_device(): lax.all_gather(jnp.dot(images, w_image, preferred_element_type=jnp.float3...  13.8 us
    unnamed x4, starting transfers between devices  10 us
    unnamed x21, local copies, waits for them, and re-layouts  3.07 us
  transfers between devices with their start and end apart: 4, of which 1 were waited for; matrix products, arithmetic and copies ran while one was open for 23% of the time, Pallas kernels for 0%

profile of v1, /device:TPU:1, one launch (start us, length us, event | category | flops | bytes accessed | tf_op | source)
XLA Modules:
  0.0 100.1 jit_solution(12646328454072607233)
XLA Ops:
  0.7 0.8 bitcast_convert_fusion
  1.5 0.7 fusion.20
  2.2 1.6 %fusion.3 = f32[24,1,288]{2,1,0:T(1,128)S(1)} fusion(bf16[1,1,24,64,288]{4,3,2,1,0:T(8,128)(2,1)} %param.8, pred[24,64,1]{1,0,2:T(8,128)(4,1)S(1)} %fusion.20), kind=kOutput, calls=%fused_computation.2 | convolution fusion | flops 884736 | bytes 913920 | tf_op jit(solution)/shard_map/bl,bld->bd/dot_general | solution.py:25
  3.8 0.3 fusion.15
  4.1 12.7 %fusion = f32[8,1536]{1,0:T(8,128)S(1)} fusion(f32[24,1536]{1,0:T(8,128)S(1)} %fusion.15), kind=kCustom, calls=%all-reduce-scatter | all-reduce-scatter fusion | flops 49153 | bytes 197120
  16.8 2.0 %collective-permute-start = (f32[6,1536]{1,0:T(8,128)S(1)}, f32[6,1536]{1,0:T(8,128)S(1)}, u32[]{:S(2)}, u32[]{:S(2)}) collective-permute-start(f32[6,1536]{1,0:T(8,128)S(1)} %slice), channel_id=1, source_target_pairs={{0,2},{2,4},{4,6},{1,3},{3,5},{5,7},{8,10},{10,12},{12,14},{9,11},... | collective-permute-start | bytes 110600
  18.9 0.3 fusion.17
  19.1 13.8 %all-gather = f32[96,1536]{1,0:T(8,128)S(1)} all-gather(f32[24,1536]{1,0:T(8,128)S(1)} %fusion.17), channel_id=2, replica_groups=mesh['loss'=4,'tower'=4,'pipe'=2] {'tower'}, dimensions={0}, use_global_device_ids=true | all-gather | bytes 737280 | tf_op jit(solution)/shard_map/all_gather | solution.py:28
  34.4 0.6 dynamic-slice.8
  35.0 0.6 dynamic-slice.16
  36.9 0.1 multiply_reduce_fusion.1
  37.1 21.1 %all-gather.1 = bf16[8,6,1536]{2,1,0:T(8,128)(2,1)S(1)} all-gather(bf16[1,6,1536]{2,1,0:T(8,128)(2,1)S(1)} %fusion.14), channel_id=1, replica_groups=mesh['loss'=4,'tower'=4,'pipe'=2] {'loss','pipe'}, dimensions={0}, use_global_device_ids=true | all-gather | bytes 165888 | tf_op jit(solution)/shard_map/all_gather | solution.py:48
  58.3 0.2 fusion.11
  58.6 0.2 convolution_multiply_fusion
  58.8 0.1 convolution_multiply_fusion.1
  59.0 10.6 %fusion.1 = f32[8,1536]{1,0:T(8,128)S(1)} fusion(f32[24,1536]{1,0:T(8,128)S(1)} %convolution_multiply_fusion.1), kind=kCustom, calls=%all-reduce-scatter.1 | all-reduce-scatter fusion | flops 49153 | bytes 197120
  69.6 1.5 %collective-permute-start.1 = (f32[6,1536]{1,0:T(8,128)S(1)}, f32[6,1536]{1,0:T(8,128)S(1)}, u32[]{:S(2)}, u32[]{:S(2)}) collective-permute-start(f32[6,1536]{1,0:T(8,128)S(1)} %slice.1), channel_id=1, source_target_pairs={{0,2},{2,4},{4,6},{1,3},{3,5},{5,7},{8,10},{10,12},{12,14},{9,11},... | collective-permute-start | bytes 110600
  71.1 20.4 %fusion.2 = f32[8,1536]{1,0:T(8,128)S(1)} fusion(f32[48,1536]{1,0:T(8,128)S(1)} %convolution_multiply_fusion), kind=kCustom, calls=%all-reduce-scatter.2 | all-reduce-scatter fusion | flops 98305 | bytes 344576
  91.5 1.9 %collective-permute-start.2 = (f32[8,1536]{1,0:T(8,128)S(1)}, f32[8,1536]{1,0:T(8,128)S(1)}, u32[]{:S(2)}, u32[]{:S(2)}) collective-permute-start(f32[8,1536]{1,0:T(8,128)S(1)} %fusion.2), channel_id=1, source_target_pairs={{0,1},{1,8},{8,9},{9,16},{16,17},{17,24},{24,25},{2,3},{3,10},{10,... | collective-permute-start | bytes 147464
  93.4 4.6 %collective-permute-start.3 = (f32[6,1536]{1,0:T(8,128)S(1)}, f32[6,1536]{1,0:T(8,128)S(1)}, u32[]{:S(2)}, u32[]{:S(2)}) collective-permute-start(f32[6,1536]{1,0:T(8,128)S(1)} %slice.2), channel_id=1, source_target_pairs={{0,8},{1,9},{8,16},{9,17},{16,24},{17,25},{2,10},{3,11},{10,18},{1... | collective-permute-start | bytes 110600
  98.2 0.7 copy.15
  98.9 0.3 collective-permute-done.3
  99.2 0.2 concatenate.2
  99.5 0.7 copy.16
  (28 shorter events, 0.7 us)
Async XLA Ops:
  0.6 18.2 %copy-start = (bf16[384,1536]{1,0:T(8,128)(2,1)S(1)}, bf16[384,1536]{1,0:T(8,128)(2,1)}, u32[]{:S(2)}) copy-start(bf16[384,1536]{1,0:T(8,128)(2,1)} %param.10) | copy-start | bytes 3538948
  0.6 3.1 %copy-start.1 = (bf16[288,1536]{1,0:T(8,128)(2,1)S(1)}, bf16[288,1536]{1,0:T(8,128)(2,1)}, u32[]{:S(2)}) copy-start(bf16[288,1536]{1,0:T(8,128)(2,1)} %param.11) | copy-start | bytes 2654212
  2.2 16.6 %copy-start.2 = (bf16[1,1,24,384]{3,2,1,0:T(8,128)(2,1)S(1)}, bf16[1,1,24,384]{3,2,1,0:T(8,128)(2,1)}, u32[]{:S(2)}) copy-start(bf16[1,1,24,384]{3,2,1,0:T(8,128)(2,1)} %param.7) | copy-start | bytes 55300
  16.8 20.0 %collective-permute-start = (f32[6,1536]{1,0:T(8,128)S(1)}, f32[6,1536]{1,0:T(8,128)S(1)}, u32[]{:S(2)}, u32[]{:S(2)}) collective-permute-start(f32[6,1536]{1,0:T(8,128)S(1)} %slice), channel_id=1, source_target_pairs={{0,2},{2,4},{4,6},{1,3},{3,5},{5,7},{8,10},{10,12},{12,14},{9,11},... | collective-permute-start | bytes 110600
  18.8 15.5 %copy-start.4 = (u32[32]{0:T(128)S(1)}, u32[32]{0:T(128)}, u32[]{:S(2)}) copy-start(u32[32]{0:T(128)} %constant.48) | copy-start | bytes 388
  18.8 16.1 %copy-start.3 = (u32[32]{0:T(128)S(1)}, u32[32]{0:T(128)}, u32[]{:S(2)}) copy-start(u32[32]{0:T(128)} %constant.56) | copy-start | bytes 388
  69.6 28.4 %collective-permute-start.1 = (f32[6,1536]{1,0:T(8,128)S(1)}, f32[6,1536]{1,0:T(8,128)S(1)}, u32[]{:S(2)}, u32[]{:S(2)}) collective-permute-start(f32[6,1536]{1,0:T(8,128)S(1)} %slice.1), channel_id=1, source_target_pairs={{0,2},{2,4},{4,6},{1,3},{3,5},{5,7},{8,10},{10,12},{12,14},{9,11},... | collective-permute-start | bytes 110600
  91.5 7.7 %collective-permute-start.2 = (f32[8,1536]{1,0:T(8,128)S(1)}, f32[8,1536]{1,0:T(8,128)S(1)}, u32[]{:S(2)}, u32[]{:S(2)}) collective-permute-start(f32[8,1536]{1,0:T(8,128)S(1)} %fusion.2), channel_id=1, source_target_pairs={{0,1},{1,8},{8,9},{9,16},{16,17},{17,24},{24,25},{2,3},{3,10},{10,... | collective-permute-start | bytes 147464
  93.4 5.8 %collective-permute-start.3 = (f32[6,1536]{1,0:T(8,128)S(1)}, f32[6,1536]{1,0:T(8,128)S(1)}, u32[]{:S(2)}, u32[]{:S(2)}) collective-permute-start(f32[6,1536]{1,0:T(8,128)S(1)} %slice.2), channel_id=1, source_target_pairs={{0,8},{1,9},{8,16},{9,17},{16,24},{17,25},{2,10},{3,11},{10,18},{1... | collective-permute-start | bytes 110600
